TPU v7x, 32 devices: a whole 2x2x4 slice. The times are simulated.
32 devices in a mesh: pts: 8 (over z, y), grp: 4 (over x, core).
Axes of the slice: x: 2, y: 2, z: 4, core: 2. Of those that a mesh axis runs over, the one named last changes fastest.
Arguments:
- jacobian: bfloat16 [32, 6, 128, 3, 256], P(('pts', 'grp')), may hold values from -0.21875 to 0.21875
- point_blocks: float32 [32, 6, 256], P(('pts', 'grp')), may hold values from -0.5 to 4, as said below
- point_grad: bfloat16 [32, 3, 256], P(('pts', 'grp')), may hold values from -6 to 6
- camera_grad: float32 [32, 128], P(('pts', 'grp')), may hold values from -6 to 6
- damping: float32 [32, 128], replicated, may hold values from 1 to 8
- incidence: int32 [32, 6], P(('pts', 'grp')), may hold values from 0 to 31, as said below
- tile_owner: int32 [8], replicated, may hold values from 0 to 7, each once
- front_first: int32 [1], replicated, may hold values from 0 to 31
Outputs:
- tiles_out: float32 [256, 128, 128], P(('pts', 'grp'))
- rhs_out: float32 [32, 128], P(('pts', 'grp'))
- front_panel: float32 [2304, 512], P(None, 'grp')
Inputs may be any that keep to these rules, and one draw needn't show every extreme that they name: `incidence`: point cluster p names 6 different camera clusters, all among (p + t) mod 32 for t from 0 to 7. `point_blocks`: each point's diagonal entries exceed the sum of the magnitudes of the two off-diagonal entries of their row by 0.1 or more. `tile_owner`: A permutation of the pts indices.
All inputs are finite; a program needn't handle non-finite values.
Results may differ from a plain program's by a relative error of at most 0.0022.
Values sent between devices are 32-bit elements; how exact they have to be, the bound alone decides.
No kernel may reach another device: no remote copies, remote signals or barrier semaphores. Data moves between devices by JAX's collectives and lax.ppermute only.
A program may use at most 128 MiB of HBM per device.

v0:
```python
import jax
import jax.numpy as jnp
import numpy as np
from jax import lax
from jax.sharding import PartitionSpec as P

TOUCH = 6
BAND = 8
FRONT = 4
PRECISE = lax.Precision.HIGHEST


def shifted(value, axis, steps):
    count = lax.axis_size(axis)
    pairs = [(source, (source + steps) % count) for source in range(count)]
    return lax.ppermute(value, axis, pairs)


def invert_blocks(blocks):
    diag_x = blocks[:, 0]
    diag_y = blocks[:, 1]
    diag_z = blocks[:, 2]
    cross_xy = blocks[:, 3]
    cross_xz = blocks[:, 4]
    cross_yz = blocks[:, 5]
    adj_xx = diag_y * diag_z - cross_yz * cross_yz
    adj_yy = diag_x * diag_z - cross_xz * cross_xz
    adj_zz = diag_x * diag_y - cross_xy * cross_xy
    adj_xy = cross_xz * cross_yz - cross_xy * diag_z
    adj_xz = cross_xy * cross_yz - diag_y * cross_xz
    adj_yz = cross_xy * cross_xz - diag_x * cross_yz
    determinant = diag_x * adj_xx + cross_xy * adj_xy + cross_xz * adj_xz
    inverse_det = 1.0 / determinant
    return [
        [adj_xx * inverse_det, adj_xy * inverse_det, adj_xz * inverse_det],
        [adj_xy * inverse_det, adj_yy * inverse_det, adj_yz * inverse_det],
        [adj_xz * inverse_det, adj_yz * inverse_det, adj_zz * inverse_det],
    ]


def scale_jacobian(jacobian, blocks):
    inverse = invert_blocks(blocks)
    widened = jacobian.astype(jnp.float32)
    columns = []
    for target in range(3):
        summed = widened[:, :, :, 0, :] * inverse[0][target][:, None, None, :]
        summed = summed + widened[:, :, :, 1, :] * inverse[1][target][:, None, None, :]
        summed = summed + widened[:, :, :, 2, :] * inverse[2][target][:, None, None, :]
        columns.append(summed)
    return jnp.stack(columns, axis=3).astype(jnp.bfloat16)


def band_table(reach_rows, reach_sum):
    row_list = []
    offset_list = []
    for row_pos in range(reach_rows):
        for offset in range(BAND):
            if row_pos + offset <= reach_sum:
                row_list.append(row_pos)
                offset_list.append(offset)
    return (np.array(row_list), np.array(offset_list))


def route_rows(tiles, tile_owner, base, row_list, offset_list, pts_count):
    offsets = BAND * row_list + offset_list
    capacity = int(offsets.max()) // pts_count + 1
    residue = jnp.mod(base + jnp.asarray(offsets), pts_count)
    target = tile_owner[residue] * capacity + jnp.asarray(offsets // pts_count)
    sending = (jnp.arange(pts_count * capacity)[:, None] == target[None, :]).astype(jnp.float32)
    return (jnp.einsum("dt,trc->drc", sending, tiles, precision=PRECISE), capacity)


def collect_rows(
    incoming, capacity, perm_inverse, anchors, usable_test, clusters, grp_count, pts_count
):
    sender = jnp.arange(pts_count * capacity) // capacity
    slot_of = jnp.arange(pts_count * capacity) % capacity
    sender_anchor = anchors(sender)
    arrived = jnp.mod(perm_inverse - BAND * sender_anchor, pts_count) + slot_of * pts_count
    row_pos = arrived // BAND
    offset = arrived % BAND
    usable = usable_test(row_pos, offset)
    home_row = jnp.mod(sender_anchor + row_pos, clusters)
    owner_slot = (BAND * home_row + offset) // pts_count
    gathering = (
        (jnp.arange(BAND * grp_count)[:, None] == owner_slot[None, :]) & usable[None, :]
    ).astype(jnp.float32)
    return jnp.einsum("ms,src->mrc", gathering, incoming, precision=PRECISE)


def per_device(
    jacobian, point_blocks, point_grad, camera_grad, damping, incidence, tile_owner, front_first
):
    pts_count = lax.axis_size("pts")
    grp_count = lax.axis_size("grp")
    clusters = pts_count * grp_count
    my_grp = lax.axis_index("grp")
    my_pts = lax.axis_index("pts")
    device = my_pts * grp_count + my_grp
    local_count = jacobian.shape[0]
    cam_rows = jacobian.shape[2]
    point_cols = 3 * jacobian.shape[4]
    window_len = 2 * BAND - 2 + FRONT
    reach = 2 * BAND - 1
    scaled = scale_jacobian(jacobian, point_blocks).reshape(
        local_count, TOUCH, cam_rows, point_cols
    )
    jac_flat = jacobian.reshape(local_count, TOUCH, cam_rows, point_cols)
    local_slot = jnp.mod(incidence - device, clusters)
    placing = (local_slot[:, None, :] == jnp.arange(BAND)[None, :, None]).astype(jnp.bfloat16)
    placed_scaled = jnp.einsum(
        "ptk,pkrx->ptrx", placing, scaled, preferred_element_type=jnp.float32
    ).astype(jnp.bfloat16)
    placed_jac = jnp.einsum(
        "ptk,pkrx->ptrx", placing, jac_flat, preferred_element_type=jnp.float32
    ).astype(jnp.bfloat16)
    band_grid = jnp.einsum(
        "ptrx,pqcx->tqrc", placed_scaled, placed_jac, preferred_element_type=jnp.float32
    )
    band_rhs = jnp.einsum(
        "ptrx,px->tr",
        placed_scaled,
        point_grad.reshape(local_count, point_cols),
        preferred_element_type=jnp.float32,
    )
    perm_inverse = jnp.sum(jnp.arange(pts_count) * (tile_owner == my_pts))
    row_list, offset_list = band_table(BAND, BAND - 1)
    band_tiles = band_grid[row_list, row_list + offset_list]
    quarters = lax.all_to_all(band_tiles, "grp", split_axis=1, concat_axis=0, tiled=True)
    reach_union = BAND + grp_count - 2
    union_rows_list, union_offsets = band_table(reach_union + 1, reach_union)
    lookup = {}
    for position in range(len(union_rows_list)):
        lookup[int(union_rows_list[position]), int(union_offsets[position])] = position
    merge_table = np.zeros((len(union_rows_list), grp_count * len(row_list)), np.float32)
    for source_grp in range(grp_count):
        for position in range(len(row_list)):
            merge_table[
                lookup[source_grp + int(row_list[position]), int(offset_list[position])],
                source_grp * len(row_list) + position,
            ] = 1.0
    union_rows = jnp.einsum("us,src->urc", jnp.asarray(merge_table), quarters, precision=PRECISE)
    outgoing, capacity = route_rows(
        union_rows, tile_owner, BAND * grp_count * my_pts, union_rows_list, union_offsets, pts_count
    )
    incoming = lax.all_to_all(outgoing, "pts", split_axis=0, concat_axis=0, tiled=True)
    owner_rows = collect_rows(
        incoming,
        capacity,
        perm_inverse,
        lambda sender: sender * grp_count,
        lambda row_pos, offset: row_pos + offset <= reach_union,
        clusters,
        grp_count,
        pts_count,
    )
    owned = lax.all_to_all(owner_rows, "grp", split_axis=0, concat_axis=1, tiled=True)
    tile_id = perm_inverse + pts_count * (BAND * my_grp + jnp.arange(BAND))
    home_row = tile_id // BAND
    offset = tile_id % BAND
    other_row = jnp.mod(home_row + offset, clusters)
    pick_damp = (home_row[:, None] == jnp.arange(clusters)[None, :]).astype(jnp.float32)
    damp_rows = jnp.dot(pick_damp, damping, precision=PRECISE)
    identity = jnp.eye(cam_rows, dtype=jnp.float32)
    owned = owned + jnp.where(
        (offset == 0)[:, None, None], damp_rows[:, :, None] * identity[None, :, :], 0.0
    )
    summed = band_rhs[0]
    for step in range(1, BAND):
        summed = summed + shifted(band_rhs[step], ("pts", "grp"), step)
    reduced = camera_grad - summed[None, :]
    front_start = front_first[0]
    window_base = front_start - (BAND - 1)
    pos_home = jnp.mod(home_row - window_base, clusters)
    pos_other = jnp.mod(other_row - window_base, clusters)
    front_axis = jnp.arange(FRONT)[:, None, None]
    reach_axis = jnp.arange(reach)[None, :, None]
    direct = (
        (pos_other[None, None, :] == BAND - 1 + front_axis)
        & (pos_home[None, None, :] == front_axis + reach_axis)
    ).astype(jnp.float32)
    mirror = (
        (pos_home[None, None, :] == BAND - 1 + front_axis)
        & (offset[None, None, :] > 0)
        & (pos_other[None, None, :] == front_axis + reach_axis)
    ).astype(jnp.float32)
    front_rows = jnp.einsum("kes,sab->keab", direct, owned, precision=PRECISE) + jnp.einsum(
        "kes,sba->keab", mirror, owned, precision=PRECISE
    )
    my_pos = jnp.mod(device - window_base, clusters)
    window_rhs = (jnp.arange(window_len)[:, None] == my_pos).astype(jnp.float32) * reduced
    front_rows, window_rhs = lax.psum((front_rows, window_rhs), ("pts", "grp"))
    flat_rows = jnp.concatenate(
        [
            front_rows.reshape(FRONT * reach, cam_rows, cam_rows),
            jnp.zeros((1, cam_rows, cam_rows), jnp.float32),
        ],
        axis=0,
    )
    lookup_table = np.full((window_len, FRONT), FRONT * reach, np.int32)
    for position in range(window_len):
        for front_pos in range(FRONT):
            if 0 <= position - front_pos < reach:
                lookup_table[position, front_pos] = front_pos * reach + position - front_pos
    columns = (
        flat_rows[lookup_table]
        .transpose(0, 2, 1, 3)
        .reshape(window_len * cam_rows, FRONT * cam_rows)
    )
    square = columns[(BAND - 1) * cam_rows : (BAND - 1 + FRONT) * cam_rows]
    factor = jnp.linalg.cholesky(square)
    panel = jax.scipy.linalg.solve_triangular(factor, columns.T, lower=True).T
    share = FRONT * cam_rows // grp_count
    front_panel = lax.dynamic_slice_in_dim(panel, my_grp * share, share, 1)
    panel_blocks = panel.reshape(window_len, cam_rows, FRONT * cam_rows)

    def inside_rest(position):
        return (position < window_len) & ((position < BAND - 1) | (position >= BAND - 1 + FRONT))

    update_mask = inside_rest(pos_home) & inside_rest(pos_other)
    pick_home = (pos_home[:, None] == jnp.arange(window_len)[None, :]).astype(jnp.float32)
    pick_other = (pos_other[:, None] == jnp.arange(window_len)[None, :]).astype(jnp.float32)
    rows_home = jnp.einsum("sp,pra->sra", pick_home, panel_blocks, precision=PRECISE)
    rows_other = jnp.einsum("sp,pra->sra", pick_other, panel_blocks, precision=PRECISE)
    change = jnp.einsum("sra,sca->src", rows_home, rows_other, precision=PRECISE)
    tiles_out = owned - jnp.where(update_mask[:, None, None], change, 0.0)
    solved_front = jax.scipy.linalg.solve_triangular(
        factor, window_rhs[BAND - 1 : BAND - 1 + FRONT].reshape(FRONT * cam_rows), lower=True
    )
    my_row = lax.dynamic_index_in_dim(
        panel_blocks, jnp.clip(my_pos, 0, window_len - 1), 0, keepdims=False
    )
    correction = reduced[0] - jnp.dot(my_row, solved_front, precision=PRECISE)
    front_piece = lax.dynamic_index_in_dim(
        solved_front.reshape(FRONT, cam_rows),
        jnp.clip(my_pos - (BAND - 1), 0, FRONT - 1),
        0,
        keepdims=False,
    )
    in_front = (my_pos >= BAND - 1) & (my_pos < BAND - 1 + FRONT)
    in_window = my_pos < window_len
    rhs_out = jnp.where(in_front, front_piece, jnp.where(in_window, correction, reduced[0]))[
        None, :
    ]
    return (tiles_out, rhs_out, front_panel)


def solution(mesh):
    in_specs = (
        P(("pts", "grp"), None, None, None, None),
        P(("pts", "grp"), None, None),
        P(("pts", "grp"), None, None),
        P(("pts", "grp"), None),
        P(),
        P(("pts", "grp"), None),
        P(),
        P(),
    )
    out_specs = (P(("pts", "grp"), None, None), P(("pts", "grp"), None), P(None, "grp"))
    return jax.shard_map(
        per_device, mesh=mesh, in_specs=in_specs, out_specs=out_specs, check_vma=False
    )
```

profile of v0, /device:TPU:0, one launch (start us, length us, event | category | flops | bytes accessed | tf_op | source)
XLA Modules:
  0.0 489.5 jit_solution(7508762552952673536)
XLA Ops:
  18.5 3.5 convolution_bitcast_fusion
  22.0 2.9 gather_fusion
  27.1 4.4 all-to-all-start
  32.1 5.0 %fusion.120 = s32[60]{0:T(128)S(1)} fusion(s32[60]{0:T(128)S(1)} %copy-done.16, s32[60]{0:T(128)S(1)} %copy-done.15, s32[]{:T(128)} %bitcast.1, s32[]{:T(128)} %bitcast.2, s32[]{:T(128)} %bitcast.3, s32[]{:T(128)} %bitcast.4, s32[]{:T(128)} %bitcast.5, s32[]{:T(128)} %bitcast.6, s32[]{:T(128)} %bitcast.7, s32[]{:T(128)} %bitcast.8, s32[]{:T(128)S(6)} %mul.589), kind=kLoop, calls=%fused_computation.234 | loop fusion | flops 1860 | bytes 756 | tf_op jit(solution)/shard_map/add | solution.py:68
  37.1 25.7 %all-to-all-done = f32[36,128,128]{2,0,1:T(8,128)S(1)} async-done(((f32[36,128,128]{2,0,1:T(8,128)}), f32[36,128,128]{2,0,1:T(8,128)S(1)}, u32[]{:S(2)}, u32[]{:S(2)}) %all-to-all-start) | async-done | bytes 2359328 | tf_op jit(solution)/shard_map/all_to_all | solution.py:129
  63.3 2.7 fusion.12
  68.2 6.6 %all-to-all-start.1 = ((f32[88,32,128]{2,1,0:T(8,128)}), f32[88,32,128]{2,1,0:T(8,128)S(1)}, u32[]{:S(2)}, u32[]{:S(2)}) async-start(f32[88,32,128]{2,1,0:T(8,128)} %copy.52), calls=%async_computation.1 | async-start | bytes 2883584 | tf_op jit(solution)/shard_map/all_to_all | solution.py:146
  78.3 30.5 %all-to-all-done.1 = f32[88,32,128]{2,1,0:T(8,128)S(1)} async-done(((f32[88,32,128]{2,1,0:T(8,128)}), f32[88,32,128]{2,1,0:T(8,128)S(1)}, u32[]{:S(2)}, u32[]{:S(2)}) %all-to-all-start.1) | async-done | bytes 1441824 | tf_op jit(solution)/shard_map/all_to_all | solution.py:146
  111.3 3.5 all-to-all-start.2
  114.8 10.1 %all-reduce.4.cloned.1.call-start = ((), (), s32[]{:S(2)}) async-start(), calls=%async_computation.3 | async-start | bytes 7864320 | tf_op jit(solution)/shard_map/psum | solution.py:192
  130.2 3.1 copy.58
  134.7 3.5 fusion.148
  151.3 38.8 %psum.15 = f32[18,128]{1,0:T(8,128)S(1)} all-reduce(f32[18,128]{1,0:T(8,128)S(1)} %broadcast_multiply_fusion), channel_id=1, replica_groups=mesh['pts'=8,'grp'=4] {'pts','grp'}, use_global_device_ids=true, to_apply=%region_10.11 | all-reduce | flops 2304 | bytes 18432 | tf_op jit(solution)/shard_map/psum | solution.py:192
  190.1 83.9 %all-reduce.4.cloned.1.call-done = f32[60,128,128]{2,1,0:T(8,128)} async-done(((f32[60,128,128]{2,1,0:T(8,128)}), f32[60,128,128]{2,1,0:T(8,128)}) %all-reduce.4.cloned.1.call-update) | async-done | bytes 3932176 | tf_op jit(solution)/shard_map/psum | solution.py:192
  274.0 4.5 concatenate.34
  278.5 5.2 %gather_fusion.1 = f32[72,128,128]{2,1,0:T(8,128)} fusion(f32[61,128,128]{2,1,0:T(8,128)} %concatenate.34, s32[1024]{0:T(1024)S(1)} %pad_clamp_fusion), kind=kCustom, calls=%fused_computation.1 | custom fusion | bytes 9437472 | tf_op jit(solution)/shard_map/gather | solution.py:206
  289.2 11.7 %cholesky.86 = f32[128,128]{1,0:T(8,128)S(1)} custom-call(f32[128,128]{1,0:T(8,128)S(1)} %cholesky.232), custom_call_target="Cholesky" | custom-call | tf_op jit(solution)/shard_map/jit(cholesky)/cholesky | solution.py:211
  301.1 6.5 %copy.75 = f32[18,128,4,128]{1,0,3,2:T(8,128)} copy(f32[18,128,4,128]{3,1,2,0:T(8,128)} %bitcast.269) | data formatting | bytes 9437184 | tf_op jit(solution)/shard_map/reshape | solution.py:208
  307.6 9.8 %custom-call.34 = f32[1,128,128]{1,2,0:T(8,128)S(1)} custom-call(f32[1,128,128]{2,1,0:T(8,128)S(1)} %get-tuple-element.50), custom_call_target="InvertDiagBlocksLowerTriangular" | custom-call | tf_op jit(solution)/shard_map/jit(cholesky)/cholesky | solution.py:211
  318.1 11.7 %cholesky.183 = f32[128,128]{1,0:T(8,128)S(1)} custom-call(f32[128,128]{1,0:T(8,128)S(1)} %cholesky.236), custom_call_target="Cholesky" | custom-call | tf_op jit(solution)/shard_map/jit(cholesky)/cholesky | solution.py:211
  331.2 9.8 %custom-call.35 = f32[1,128,128]{1,2,0:T(8,128)S(1)} custom-call(f32[1,128,128]{2,1,0:T(8,128)S(1)} %get-tuple-element.47), custom_call_target="InvertDiagBlocksLowerTriangular" | custom-call | tf_op jit(solution)/shard_map/jit(cholesky)/cholesky | solution.py:211
  341.6 12.1 %cholesky.204 = f32[128,128]{1,0:T(8,128)S(1)} custom-call(f32[128,128]{1,0:T(8,128)S(1)} %cholesky.241), custom_call_target="Cholesky" | custom-call | tf_op jit(solution)/shard_map/jit(cholesky)/cholesky | solution.py:211
  354.4 9.8 %custom-call.36 = f32[1,128,128]{1,2,0:T(8,128)S(1)} custom-call(f32[1,128,128]{2,1,0:T(8,128)S(1)} %get-tuple-element.44), custom_call_target="InvertDiagBlocksLowerTriangular" | custom-call | tf_op jit(solution)/shard_map/jit(cholesky)/cholesky | solution.py:211
  364.8 11.7 %cholesky.221 = f32[128,128]{1,0:T(8,128)S(1)} custom-call(f32[128,128]{1,0:T(8,128)S(1)} %convolution_subtract_fusion.5), custom_call_target="Cholesky" | custom-call | tf_op jit(solution)/shard_map/jit(cholesky)/cholesky | solution.py:211
  379.9 8.0 %while.1 = (s32[]{:T(128)}, f32[512,512]{1,0:T(8,128)S(1)}, s32[4,2]{0,1:T(2,128)S(1)}, f32[4,128,128]{2,1,0:T(8,128)S(1)}, s32[]{:T(128)}) while((s32[]{:T(128)}, f32[512,512]{1,0:T(8,128)S(1)}, s32[4,2]{0,1:T(2,128)S(1)}, f32[4,128,128]{2,1,0:T(8,128)S(1)}, s32[]{:T(128)}) %tuple.64), condition=%wide.while_cond, body=%wide.while_body.sunk | while | flops 2 | bytes 131181 | solution.py:212
  387.9 39.5 %custom-call.37 = f32[4,128,128]{1,2,0:T(8,128)S(1)} custom-call(f32[4,128,128]{2,1,0:T(8,128)S(1)} %get-tuple-element.10), custom_call_target="InvertDiagBlocksLowerTriangular" | custom-call | tf_op jit(solution)/shard_map/jit(_solve_triangular)/triangular_solve | solution.py:212
  427.4 3.8 copy.113
  440.6 4.3 pad_maximum_fusion
  444.9 6.1 %copy.63 = f32[2304,512]{1,0:T(8,128)} copy(f32[2304,512]{0,1:T(8,128)} %get-tuple-element.37) | data formatting | bytes 9437184 | tf_op jit(solution)/shard_map/transpose | solution.py:212
  451.0 7.7 %fusion.2 = f32[8,128,512]{2,0,1:T(8,128)S(1)} fusion(f32[18,128,512]{2,1,0:T(8,128)} %bitcast.264, s32[8]{0:T(128)S(1)} %get-tuple-element.30), kind=kOutput, calls=%fused_computation.6 | convolution fusion | flops 113246352 | bytes 6815776 | tf_op jit(solution)/shard_map/sp,pra->sra/dot_general | solution.py:223
  458.6 5.9 %fusion = f32[8,128,512]{2,0,1:T(8,128)} fusion(f32[18,128,512]{2,1,0:T(8,128)S(1)} %bitcast.266, s32[8]{0:T(128)S(1)} %get-tuple-element.29), kind=kOutput, calls=%fused_computation.4 | convolution fusion | flops 113246352 | bytes 6815776 | tf_op jit(solution)/shard_map/sp,pra->sra/dot_general | solution.py:224
  473.8 6.7 %fusion.28 = f32[8,128,128]{2,1,0:T(8,128)} fusion(f32[8,128,128]{2,1,0:T(8,128)S(1)} %bitcast_add_fusion.2, f32[8,128,512]{2,0,1:T(8,128)} %fusion, f32[8,128,512]{2,0,1:T(8,128)S(1)} %fusion.2, pred[8]{0:T(512)(128)(4,1)S(1)} %get-tuple-element.28), kind=kOutput, calls=%fused_computation.37 | convolution fusion | flops 805568512 | bytes 5242888 | tf_op jit(solution)/shard_map/sra,sca->src/dot_general | solution.py:225
  (150 shorter events, 80.4 us)
Async XLA Ops:
  7.2 118.4 %copy-start = (f32[32,128]{1,0:T(8,128)S(1)}, f32[32,128]{1,0:T(8,128)}, u32[]{:S(2)}) copy-start(f32[32,128]{1,0:T(8,128)} %param.21) | copy-start | bytes 49156
  13.8 2.0 copy-start.17
  15.8 1.4 copy-start.5
  17.2 1.2 copy-start.3
  18.5 3.5 copy-start.9
  27.1 4.4 copy-start.11
  27.1 5.0 %copy-start.15 = (s32[60]{0:T(128)S(1)}, s32[60]{0:T(128)}, u32[]{:S(2)}) copy-start(s32[60]{0:T(128)} %constant.368.clone) | copy-start | bytes 724
  27.1 5.0 %copy-start.16 = (s32[60]{0:T(128)S(1)}, s32[60]{0:T(128)}, u32[]{:S(2)}) copy-start(s32[60]{0:T(128)} %constant.369.clone) | copy-start | bytes 724
  27.1 35.7 %all-to-all-start = ((f32[36,128,128]{2,0,1:T(8,128)}), f32[36,128,128]{2,0,1:T(8,128)S(1)}, u32[]{:S(2)}, u32[]{:S(2)}) async-start(f32[36,128,128]{2,0,1:T(8,128)} %copy.49), calls=%async_computation | async-start | bytes 5242880 | tf_op jit(solution)/shard_map/all_to_all | solution.py:129
  37.1 26.2 %copy-start.10 = (f32[60,144,1]{1,0,2:T(8,128)S(1)}, f32[60,144,1]{1,0,2:T(8,128)}, u32[]{:S(2)}) copy-start(f32[60,144,1]{1,0,2:T(8,128)} %constant.431) | copy-start | bytes 103684
  68.2 40.5 %all-to-all-start.1 = ((f32[88,32,128]{2,1,0:T(8,128)}), f32[88,32,128]{2,1,0:T(8,128)S(1)}, u32[]{:S(2)}, u32[]{:S(2)}) async-start(f32[88,32,128]{2,1,0:T(8,128)} %copy.52), calls=%async_computation.1 | async-start | bytes 2883584 | tf_op jit(solution)/shard_map/all_to_all | solution.py:146
  111.3 14.4 %all-to-all-start.2 = ((f32[32,32,128]{2,1,0:T(8,128)}), f32[32,32,128]{2,1,0:T(8,128)S(1)}, u32[]{:S(2)}, u32[]{:S(2)}) async-start(f32[32,32,128]{2,1,0:T(8,128)} %copy.54), calls=%async_computation.2 | async-start | bytes 1048576 | tf_op jit(solution)/shard_map/all_to_all | solution.py:157
  114.8 159.2 %all-reduce.4.cloned.1.call-start = ((), (), s32[]{:S(2)}) async-start(), calls=%async_computation.3 | async-start | bytes 7864320 | tf_op jit(solution)/shard_map/psum | solution.py:192
  133.3 0.7 copy-start.12
  133.3 1.4 copy-start.4
  133.9 8.4 %copy-start.14 = (s32[72]{0:T(128)S(1)}, s32[72]{0:T(128)}, u32[]{:S(2)}) copy-start(s32[72]{0:T(128)} %constant.430) | copy-start | bytes 868
  133.9 17.3 %copy-start.13 = (f32[1,128]{1,0:T(1,128)S(1)}, f32[1,128]{1,0:T(1,128)}, u32[]{:S(2)}) copy-start(f32[1,128]{1,0:T(1,128)} %param.20) | copy-start | bytes 1540
  138.3 6.6 %collective-permute-start = (f32[128]{0:T(128)S(1)}, f32[128]{0:T(128)S(1)}, u32[]{:S(2)}, u32[]{:S(2)}) collective-permute-start(f32[128]{0:T(128)S(1)} %get-tuple-element.57), channel_id=1, source_target_pairs={{0,1},{1,2},{2,3},{3,4},{4,5},{5,6},{6,7},{7,8},{8,9},{9,10},{10,1... | collective-permute-start | bytes 1544 | tf_op jit(solution)/shard_map/ppermute | solution.py:16
  138.5 7.3 %collective-permute-start.1 = (f32[128]{0:T(128)S(1)}, f32[128]{0:T(128)S(1)}, u32[]{:S(2)}, u32[]{:S(2)}) collective-permute-start(f32[128]{0:T(128)S(1)} %get-tuple-element.63), channel_id=1, source_target_pairs={{0,2},{1,3},{2,4},{3,5},{4,6},{5,7},{6,8},{7,9},{8,10},{9,11},{10,... | collective-permute-start | bytes 1544 | tf_op jit(solution)/shard_map/ppermute | solution.py:16
  140.1 7.4 %collective-permute-start.2 = (f32[128]{0:T(128)S(1)}, f32[128]{0:T(128)S(1)}, u32[]{:S(2)}, u32[]{:S(2)}) collective-permute-start(f32[128]{0:T(128)S(1)} %get-tuple-element.62), channel_id=1, source_target_pairs={{0,3},{1,4},{2,5},{3,6},{4,7},{5,8},{6,9},{7,10},{8,11},{9,12},{10... | collective-permute-start | bytes 1544 | tf_op jit(solution)/shard_map/ppermute | solution.py:16
  142.3 6.3 %collective-permute-start.3 = (f32[128]{0:T(128)S(1)}, f32[128]{0:T(128)S(1)}, u32[]{:S(2)}, u32[]{:S(2)}) collective-permute-start(f32[128]{0:T(128)S(1)} %get-tuple-element.61), channel_id=1, source_target_pairs={{0,4},{1,5},{2,6},{3,7},{4,8},{5,9},{6,10},{7,11},{8,12},{9,13},{1... | collective-permute-start | bytes 1544 | tf_op jit(solution)/shard_map/ppermute | solution.py:16
  142.3 6.3 %collective-permute-start.4 = (f32[128]{0:T(128)S(1)}, f32[128]{0:T(128)S(1)}, u32[]{:S(2)}, u32[]{:S(2)}) collective-permute-start(f32[128]{0:T(128)S(1)} %get-tuple-element.60), channel_id=1, source_target_pairs={{0,5},{1,6},{2,7},{3,8},{4,9},{5,10},{6,11},{7,12},{8,13},{9,14},{... | collective-permute-start | bytes 1544 | tf_op jit(solution)/shard_map/ppermute | solution.py:16
  144.9 6.3 %collective-permute-start.5 = (f32[128]{0:T(128)S(1)}, f32[128]{0:T(128)S(1)}, u32[]{:S(2)}, u32[]{:S(2)}) collective-permute-start(f32[128]{0:T(128)S(1)} %get-tuple-element.59), channel_id=1, source_target_pairs={{0,6},{1,7},{2,8},{3,9},{4,10},{5,11},{6,12},{7,13},{8,14},{9,15},... | collective-permute-start | bytes 1544 | tf_op jit(solution)/shard_map/ppermute | solution.py:16
  145.8 5.4 %collective-permute-start.6 = (f32[128]{0:T(128)S(1)}, f32[128]{0:T(128)S(1)}, u32[]{:S(2)}, u32[]{:S(2)}) collective-permute-start(f32[128]{0:T(128)S(1)} %get-tuple-element.58), channel_id=1, source_target_pairs={{0,7},{1,8},{2,9},{3,10},{4,11},{5,12},{6,13},{7,14},{8,15},{9,16}... | collective-permute-start | bytes 1544 | tf_op jit(solution)/shard_map/ppermute | solution.py:16
  288.2 1.0 copy-start.7
  301.1 16.4 %copy-start.8 = (f32[512,512]{1,0:T(8,128)S(1)}, f32[512,512]{1,0:T(8,128)}, u32[]{:S(2)}) copy-start(f32[512,512]{1,0:T(8,128)} %copy-done.7) | copy-start | bytes 3145732
  387.9 49.3 %copy-start.6 = (f32[512,512]{1,0:T(8,128)}, f32[512,512]{1,0:T(8,128)S(1)}, u32[]{:S(2)}) copy-start(f32[512,512]{1,0:T(8,128)S(1)} %get-tuple-element.133) | copy-start | bytes 3145732
  451.0 7.7 %copy-start.2 = (f32[2304,512]{1,0:T(8,128)S(1)}, f32[2304,512]{1,0:T(8,128)}, u32[]{:S(2)}) copy-start(f32[2304,512]{1,0:T(8,128)} %copy.63) | copy-start | bytes 14155780
  473.8 8.5 %copy-start.1 = (f32[32,128]{1,0:T(8,128)S(1)}, f32[32,128]{1,0:T(8,128)}, u32[]{:S(2)}) copy-start(f32[32,128]{1,0:T(8,128)} %param.21) | copy-start | bytes 49156
Sparse Core Ops, SparseCore 0:
  133.4 140.5 all-reduce.3
where the time goes:
time: 499 us; the launch traced here: 490 us
  waiting for transfers between devices  147 us (29%)
  other arithmetic  134 us (27%)
  local copies, waits for them, and re-layouts  66.2 us (13%)
  matrix products  54.6 us (11%)
  blocking collectives  38.8 us (8%)
  starting transfers between devices  30.4 us (6%)
  between operations  18.1 us (4%)
    psum x1, waiting for transfers between devices, per_device(): front_rows, window_rhs = lax.psum((front_rows, window_rhs), ('pts', 'grp'))  83.9 us
    another operation x15, other arithmetic, per_device(): factor = jnp.linalg.cholesky(square)  79.4 us
    another operation x4, other arithmetic, per_device(): panel = jax.scipy.linalg.solve_triangular(factor, columns.T, lower=True).T  43.9 us
    psum x1, blocking collectives, per_device(): front_rows, window_rhs = lax.psum((front_rows, window_rhs), ('pts', 'grp'))  38.8 us
    all_to_all x1, waiting for transfers between devices, per_device(): lax.all_to_all(outgoing, 'pts', split_axis=0, concat_axis=0, tiled=True)  30.5 us
    all_to_all x1, waiting for transfers between devices, per_device(): lax.all_to_all(band_tiles, 'grp', split_axis=1, concat_axis=0, tiled=True)  25.7 us
    unnamed x40, local copies, waits for them, and re-layouts  13.1 us
    psum x1, starting transfers between devices, per_device(): front_rows, window_rhs = lax.psum((front_rows, window_rhs), ('pts', 'grp'))  10.1 us
  transfers between devices with their start and end apart: 11, of which 7 were waited for; matrix products, arithmetic and copies ran while one was open for 3% of the time, Pallas kernels for 0%

commit v1 on v0

--- a/solution.py
+++ b/solution.py
@@ -8,6 +8,17 @@
 BAND = 8
 FRONT = 4
 PRECISE = lax.Precision.HIGHEST
+
+
+def split_up(value, dim, size):
+    before, after = (value.shape[:dim], value.shape[dim + 1 :])
+    return jnp.moveaxis(value.reshape(*before, size, -1, *after), dim, 0)
+
+
+def in_order(pieces, dim):
+    shape = list(pieces.shape[1:])
+    shape[dim] *= pieces.shape[0]
+    return jnp.moveaxis(pieces, 0, dim).reshape(shape)
 
 
 def shifted(value, axis, steps):
@@ -143,7 +154,15 @@
     outgoing, capacity = route_rows(
         union_rows, tile_owner, BAND * grp_count * my_pts, union_rows_list, union_offsets, pts_count
     )
-    incoming = lax.all_to_all(outgoing, "pts", split_axis=0, concat_axis=0, tiled=True)
+    devices, place = (lax.axis_size("pts"), lax.axis_index("pts"))
+    pieces = split_up(outgoing, 0, devices)
+    result = pieces
+    for k in range(1, devices):
+        target_2, source_2 = ((place + k) % devices, (place - k) % devices)
+        sent = lax.dynamic_index_in_dim(pieces, target_2, 0)
+        received = lax.ppermute(sent, "pts", [(i, (i + k) % devices) for i in range(devices)])
+        result = lax.dynamic_update_slice_in_dim(result, received, source_2, axis=0)
+    incoming = in_order(result, 0)
     owner_rows = collect_rows(
         incoming,
         capacity,

time: 499 us -> 500 us (level)
  starting transfers between devices: 30.4 us -> 47.3 us
  waiting for transfers between devices: 147 us -> 134 us
    all_to_all x1 -> x0, waiting for transfers between devices: 30.5 us -> none  [per_device(): lax.all_to_all(outgoing, 'pts', split_axis=0, concat_axis=0, tiled=True)]
    ppermute x0 -> x7, starting transfers between devices: none -> 21.6 us  [per_device(): lax.ppermute(sent, 'pts', [(i, (i + k) % devices) for i in range(devices)])]
    ppermute x0 -> x7, waiting for transfers between devices: none -> 12.5 us  [per_device(): lax.ppermute(sent, 'pts', [(i, (i + k) % devices) for i in range(devices)])]
    ppermute x7, starting transfers between devices: 5.81 us -> 17.8 us  [shifted(): return lax.ppermute(value, axis, pairs)]
    psum x1, starting transfers between devices: 10.1 us -> 0.04 us  [per_device(): front_rows, window_rhs = lax.psum((front_rows, window_rhs), ('pts', 'grp'))]
    all_to_all x1, waiting for transfers between devices: 0.01 us -> 7.88 us  [per_device(): lax.all_to_all(owner_rows, 'grp', split_axis=0, concat_axis=1, tiled=True)]
    all_to_all x1 -> x0, starting transfers between devices: 6.65 us -> none  [per_device(): lax.all_to_all(outgoing, 'pts', split_axis=0, concat_axis=0, tiled=True)]
  transfers between devices with their start and end apart: 11 -> 17, of which waited for: 7 -> 9; matrix products, arithmetic and copies ran while one was open for 3% -> 3% of each run, Pallas kernels for 0% -> 0%
where the time goes in v1:
time: 500 us; the launch traced here: 492 us
  other arithmetic  134 us (27%)
  waiting for transfers between devices  134 us (27%)
  local copies, waits for them, and re-layouts  65.5 us (13%)
  matrix products  54.6 us (11%)
  starting transfers between devices  47.3 us (9%)
  blocking collectives  37 us (7%)
  between operations  18.5 us (4%)
    psum x1, waiting for transfers between devices, per_device(): front_rows, window_rhs = lax.psum((front_rows, window_rhs), ('pts', 'grp'))  85.1 us
    another operation x15, other arithmetic, per_device(): factor = jnp.linalg.cholesky(square)  79.2 us
    another operation x4, other arithmetic, per_device(): panel = jax.scipy.linalg.solve_triangular(factor, columns.T, lower=True).T  43.9 us
    psum x1, blocking collectives, per_device(): front_rows, window_rhs = lax.psum((front_rows, window_rhs), ('pts', 'grp'))  37 us
    all_to_all x1, waiting for transfers between devices, per_device(): lax.all_to_all(band_tiles, 'grp', split_axis=1, concat_axis=0, tiled=True)  23.5 us
    ppermute x7, starting transfers between devices, per_device(): lax.ppermute(sent, 'pts', [(i, (i + k) % devices) for i in range(devices)])  21.6 us
    ppermute x7, starting transfers between devices, shifted(): return lax.ppermute(value, axis, pairs)  17.8 us
    unnamed x40, local copies, waits for them, and re-layouts  13.1 us
  transfers between devices with their start and end apart: 17, of which 9 were waited for; matrix products, arithmetic and copies ran while one was open for 3% of the time, Pallas kernels for 0%

profile of v1, /device:TPU:0, one launch (start us, length us, event | category | flops | bytes accessed | tf_op | source)
XLA Modules:
  0.0 491.6 jit_solution(8358686760833284133)
XLA Ops:
  27.1 4.4 all-to-all-start
  34.3 5.1 %fusion.120 = s32[60]{0:T(128)S(1)} fusion(s32[60]{0:T(128)S(1)} %copy-done.16, s32[60]{0:T(128)S(1)} %copy-done.15, s32[]{:T(128)} %bitcast.1, s32[]{:T(128)} %bitcast.2, s32[]{:T(128)} %bitcast.3, s32[]{:T(128)} %bitcast.4, s32[]{:T(128)} %bitcast.5, s32[]{:T(128)} %bitcast.6, s32[]{:T(128)} %bitcast.7, s32[]{:T(128)} %bitcast.8, s32[]{:T(128)S(6)} %mul.589), kind=kLoop, calls=%fused_computation.248 | loop fusion | flops 1860 | bytes 756 | tf_op jit(solution)/shard_map/add | solution.py:79
  39.3 23.5 %all-to-all-done = f32[36,128,128]{2,0,1:T(8,128)S(1)} async-done(((f32[36,128,128]{2,0,1:T(8,128)}), f32[36,128,128]{2,0,1:T(8,128)S(1)}, u32[]{:S(2)}, u32[]{:S(2)}) %all-to-all-start) | async-done | bytes 2359328 | tf_op jit(solution)/shard_map/all_to_all | solution.py:140
  69.6 7.2 %collective-permute-done = f32[1,11,32,128]{3,2,1,0:T(8,128)S(1)} collective-permute-done((f32[1,11,32,128]{3,2,1,0:T(8,128)S(1)}, f32[1,11,32,128]{3,2,1,0:T(8,128)S(1)}, u32[]{:S(2)}, u32[]{:S(2)}) %collective-permute-start) | collective-permute-done | bytes 180256 | tf_op jit(solution)/shard_map/ppermute | solution.py:163
  81.0 3.5 collective-permute-start.4
  86.4 11.4 %collective-permute-start.6 = (f32[1,11,32,128]{3,2,1,0:T(8,128)S(1)}, f32[1,11,32,128]{3,2,1,0:T(8,128)S(1)}, u32[]{:S(2)}, u32[]{:S(2)}) collective-permute-start(f32[1,11,32,128]{3,2,1,0:T(8,128)S(1)} %get-tuple-element.41), channel_id=1, source_target_pairs={{0,28},{4,0},{8,4},{12,8},{16,12},{20,16},{24,20},{28,24},{1,29},{... | collective-permute-start | bytes 540680 | tf_op jit(solution)/shard_map/ppermute | solution.py:163
  109.8 7.9 %all-to-all-done.1 = f32[32,32,128]{2,1,0:T(8,128)S(1)} async-done(((f32[32,32,128]{2,1,0:T(8,128)}), f32[32,32,128]{2,1,0:T(8,128)S(1)}, u32[]{:S(2)}, u32[]{:S(2)}) %all-to-all-start.1) | async-done | bytes 524320 | tf_op jit(solution)/shard_map/all_to_all | solution.py:176
  126.7 3.5 fusion.148
  130.3 5.9 %collective-permute-start.10 = (f32[128]{0:T(128)S(1)}, f32[128]{0:T(128)S(1)}, u32[]{:S(2)}, u32[]{:S(2)}) collective-permute-start(f32[128]{0:T(128)S(1)} %get-tuple-element.68), channel_id=1, source_target_pairs={{0,4},{1,5},{2,6},{3,7},{4,8},{5,9},{6,10},{7,11},{8,12},{9,13},{1... | collective-permute-start | bytes 1544 | tf_op jit(solution)/shard_map/ppermute | solution.py:27
  136.1 5.1 %collective-permute-start.12 = (f32[128]{0:T(128)S(1)}, f32[128]{0:T(128)S(1)}, u32[]{:S(2)}, u32[]{:S(2)}) collective-permute-start(f32[128]{0:T(128)S(1)} %get-tuple-element.66), channel_id=1, source_target_pairs={{0,6},{1,7},{2,8},{3,9},{4,10},{5,11},{6,12},{7,13},{8,14},{9,15},... | collective-permute-start | bytes 1544 | tf_op jit(solution)/shard_map/ppermute | solution.py:27
  141.3 5.0 %collective-permute-start.13 = (f32[128]{0:T(128)S(1)}, f32[128]{0:T(128)S(1)}, u32[]{:S(2)}, u32[]{:S(2)}) collective-permute-start(f32[128]{0:T(128)S(1)} %get-tuple-element.65), channel_id=1, source_target_pairs={{0,7},{1,8},{2,9},{3,10},{4,11},{5,12},{6,13},{7,14},{8,15},{9,16}... | collective-permute-start | bytes 1544 | tf_op jit(solution)/shard_map/ppermute | solution.py:27
  148.2 4.7 collective-permute-done.7
  153.7 37.0 %psum.15 = f32[18,128]{1,0:T(8,128)S(1)} all-reduce(f32[18,128]{1,0:T(8,128)S(1)} %broadcast_multiply_fusion), channel_id=1, replica_groups=mesh['pts'=8,'grp'=4] {'pts','grp'}, use_global_device_ids=true, to_apply=%region_10.11 | all-reduce | flops 2304 | bytes 18432 | tf_op jit(solution)/shard_map/psum | solution.py:211
  190.7 85.1 %all-reduce.4.cloned.1.call-done = f32[60,128,128]{2,1,0:T(8,128)} async-done(((f32[60,128,128]{2,1,0:T(8,128)}), f32[60,128,128]{2,1,0:T(8,128)}) %all-reduce.4.cloned.1.call-update) | async-done | bytes 3932176 | tf_op jit(solution)/shard_map/psum | solution.py:211
  275.8 4.5 concatenate.34
  280.4 5.2 %gather_fusion.1 = f32[72,128,128]{2,1,0:T(8,128)} fusion(f32[61,128,128]{2,1,0:T(8,128)} %concatenate.34, s32[1024]{0:T(1024)S(1)} %pad_clamp_fusion), kind=kCustom, calls=%fused_computation.1 | custom fusion | bytes 9437472 | tf_op jit(solution)/shard_map/gather | solution.py:225
  291.1 11.7 %cholesky.86 = f32[128,128]{1,0:T(8,128)S(1)} custom-call(f32[128,128]{1,0:T(8,128)S(1)} %cholesky.232), custom_call_target="Cholesky" | custom-call | tf_op jit(solution)/shard_map/jit(cholesky)/cholesky | solution.py:230
  303.0 6.7 %copy.77 = f32[18,128,4,128]{1,0,3,2:T(8,128)} copy(f32[18,128,4,128]{3,1,2,0:T(8,128)} %bitcast.271) | data formatting | bytes 9437184 | tf_op jit(solution)/shard_map/reshape | solution.py:227
  309.7 9.8 %custom-call.34 = f32[1,128,128]{1,2,0:T(8,128)S(1)} custom-call(f32[1,128,128]{2,1,0:T(8,128)S(1)} %get-tuple-element.57), custom_call_target="InvertDiagBlocksLowerTriangular" | custom-call | tf_op jit(solution)/shard_map/jit(cholesky)/cholesky | solution.py:230
  320.2 11.7 %cholesky.183 = f32[128,128]{1,0:T(8,128)S(1)} custom-call(f32[128,128]{1,0:T(8,128)S(1)} %cholesky.236), custom_call_target="Cholesky" | custom-call | tf_op jit(solution)/shard_map/jit(cholesky)/cholesky | solution.py:230
  333.2 9.8 %custom-call.35 = f32[1,128,128]{1,2,0:T(8,128)S(1)} custom-call(f32[1,128,128]{2,1,0:T(8,128)S(1)} %get-tuple-element.54), custom_call_target="InvertDiagBlocksLowerTriangular" | custom-call | tf_op jit(solution)/shard_map/jit(cholesky)/cholesky | solution.py:230
  343.7 11.9 %cholesky.204 = f32[128,128]{1,0:T(8,128)S(1)} custom-call(f32[128,128]{1,0:T(8,128)S(1)} %cholesky.241), custom_call_target="Cholesky" | custom-call | tf_op jit(solution)/shard_map/jit(cholesky)/cholesky | solution.py:230
  356.2 9.8 %custom-call.36 = f32[1,128,128]{1,2,0:T(8,128)S(1)} custom-call(f32[1,128,128]{2,1,0:T(8,128)S(1)} %get-tuple-element.51), custom_call_target="InvertDiagBlocksLowerTriangular" | custom-call | tf_op jit(solution)/shard_map/jit(cholesky)/cholesky | solution.py:230
  366.7 11.7 %cholesky.221 = f32[128,128]{1,0:T(8,128)S(1)} custom-call(f32[128,128]{1,0:T(8,128)S(1)} %convolution_subtract_fusion.5), custom_call_target="Cholesky" | custom-call | tf_op jit(solution)/shard_map/jit(cholesky)/cholesky | solution.py:230
  381.9 8.0 %while.1 = (s32[]{:T(128)}, f32[512,512]{1,0:T(8,128)S(1)}, s32[4,2]{0,1:T(2,128)S(1)}, f32[4,128,128]{2,1,0:T(8,128)S(1)}, s32[]{:T(128)}) while((s32[]{:T(128)}, f32[512,512]{1,0:T(8,128)S(1)}, s32[4,2]{0,1:T(2,128)S(1)}, f32[4,128,128]{2,1,0:T(8,128)S(1)}, s32[]{:T(128)}) %tuple.70), condition=%wide.while_cond, body=%wide.while_body.sunk | while | flops 2 | bytes 131181 | solution.py:231
  389.9 39.5 %custom-call.37 = f32[4,128,128]{1,2,0:T(8,128)S(1)} custom-call(f32[4,128,128]{2,1,0:T(8,128)S(1)} %get-tuple-element.10), custom_call_target="InvertDiagBlocksLowerTriangular" | custom-call | tf_op jit(solution)/shard_map/jit(_solve_triangular)/triangular_solve | solution.py:231
  429.5 3.8 copy.115
  442.7 4.2 pad_maximum_fusion
  446.9 6.1 %copy.65 = f32[2304,512]{1,0:T(8,128)} copy(f32[2304,512]{0,1:T(8,128)} %get-tuple-element.37) | data formatting | bytes 9437184 | tf_op jit(solution)/shard_map/transpose | solution.py:231
  453.0 7.7 %fusion.2 = f32[8,128,512]{2,0,1:T(8,128)S(1)} fusion(f32[18,128,512]{2,1,0:T(8,128)} %bitcast.266, s32[8]{0:T(128)S(1)} %get-tuple-element.30), kind=kOutput, calls=%fused_computation.6 | convolution fusion | flops 113246352 | bytes 6815776 | tf_op jit(solution)/shard_map/sp,pra->sra/dot_general | solution.py:242
  460.7 5.9 %fusion = f32[8,128,512]{2,0,1:T(8,128)} fusion(f32[18,128,512]{2,1,0:T(8,128)S(1)} %bitcast.268, s32[8]{0:T(128)S(1)} %get-tuple-element.29), kind=kOutput, calls=%fused_computation.4 | convolution fusion | flops 113246352 | bytes 6815776 | tf_op jit(solution)/shard_map/sp,pra->sra/dot_general | solution.py:243
  475.8 6.7 %fusion.28 = f32[8,128,128]{2,1,0:T(8,128)} fusion(f32[8,128,128]{2,1,0:T(8,128)S(1)} %bitcast_add_fusion.2, f32[8,128,512]{2,0,1:T(8,128)} %fusion, f32[8,128,512]{2,0,1:T(8,128)S(1)} %fusion.2, pred[8]{0:T(512)(128)(4,1)S(1)} %get-tuple-element.28), kind=kOutput, calls=%fused_computation.37 | convolution fusion | flops 805568512 | bytes 5242888 | tf_op jit(solution)/shard_map/sra,sca->src/dot_general | solution.py:244
  (170 shorter events, 96.8 us)
Async XLA Ops:
  7.2 102.5 %copy-start = (f32[32,128]{1,0:T(8,128)S(1)}, f32[32,128]{1,0:T(8,128)}, u32[]{:S(2)}) copy-start(f32[32,128]{1,0:T(8,128)} %param.21) | copy-start | bytes 49156
  13.8 2.0 copy-start.17
  15.8 1.4 copy-start.5
  18.5 3.5 copy-start.9
  27.1 5.1 %copy-start.11 = (s32[8]{0:T(128)S(1)}, s32[8]{0:T(128)}, u32[]{:S(2)}) copy-start(s32[8]{0:T(128)} %param.23) | copy-start | bytes 100
  27.1 7.1 %copy-start.15 = (s32[60]{0:T(128)S(1)}, s32[60]{0:T(128)}, u32[]{:S(2)}) copy-start(s32[60]{0:T(128)} %constant.459.clone) | copy-start | bytes 724
  27.1 7.1 %copy-start.16 = (s32[60]{0:T(128)S(1)}, s32[60]{0:T(128)}, u32[]{:S(2)}) copy-start(s32[60]{0:T(128)} %constant.460.clone) | copy-start | bytes 724
  27.1 35.7 %all-to-all-start = ((f32[36,128,128]{2,0,1:T(8,128)}), f32[36,128,128]{2,0,1:T(8,128)S(1)}, u32[]{:S(2)}, u32[]{:S(2)}) async-start(f32[36,128,128]{2,0,1:T(8,128)} %copy.51), calls=%async_computation | async-start | bytes 5242880 | tf_op jit(solution)/shard_map/all_to_all | solution.py:140
  39.3 24.0 %copy-start.10 = (f32[60,144,1]{1,0,2:T(8,128)S(1)}, f32[60,144,1]{1,0,2:T(8,128)}, u32[]{:S(2)}) copy-start(f32[60,144,1]{1,0,2:T(8,128)} %constant.522) | copy-start | bytes 103684
  67.2 9.7 %collective-permute-start = (f32[1,11,32,128]{3,2,1,0:T(8,128)S(1)}, f32[1,11,32,128]{3,2,1,0:T(8,128)S(1)}, u32[]{:S(2)}, u32[]{:S(2)}) collective-permute-start(f32[1,11,32,128]{3,2,1,0:T(8,128)S(1)} %constant_dynamic-slice_fusion.8), channel_id=1, source_target_pairs={{0,4},{4,8},{8,12},{12,16},{16,20},{20,24},{24,28},{28,0},{1,5},{5... | collective-permute-start | bytes 540680 | tf_op jit(solution)/shard_map/ppermute | solution.py:163
  77.0 9.4 %collective-permute-start.1 = (f32[1,11,32,128]{3,2,1,0:T(8,128)S(1)}, f32[1,11,32,128]{3,2,1,0:T(8,128)S(1)}, u32[]{:S(2)}, u32[]{:S(2)}) collective-permute-start(f32[1,11,32,128]{3,2,1,0:T(8,128)S(1)} %get-tuple-element.46), channel_id=1, source_target_pairs={{0,8},{4,12},{8,16},{12,20},{16,24},{20,28},{24,0},{28,4},{1,9},{5... | collective-permute-start | bytes 540680 | tf_op jit(solution)/shard_map/ppermute | solution.py:163
  77.7 20.1 %collective-permute-start.2 = (f32[1,11,32,128]{3,2,1,0:T(8,128)S(1)}, f32[1,11,32,128]{3,2,1,0:T(8,128)S(1)}, u32[]{:S(2)}, u32[]{:S(2)}) collective-permute-start(f32[1,11,32,128]{3,2,1,0:T(8,128)S(1)} %get-tuple-element.45), channel_id=1, source_target_pairs={{0,12},{4,16},{8,20},{12,24},{16,28},{20,0},{24,4},{28,8},{1,13},{... | collective-permute-start | bytes 540680 | tf_op jit(solution)/shard_map/ppermute | solution.py:163
  79.7 20.2 %collective-permute-start.3 = (f32[1,11,32,128]{3,2,1,0:T(8,128)S(1)}, f32[1,11,32,128]{3,2,1,0:T(8,128)S(1)}, u32[]{:S(2)}, u32[]{:S(2)}) collective-permute-start(f32[1,11,32,128]{3,2,1,0:T(8,128)S(1)} %get-tuple-element.44), channel_id=1, source_target_pairs={{0,16},{4,20},{8,24},{12,28},{16,0},{20,4},{24,8},{28,12},{1,17},{... | collective-permute-start | bytes 540680 | tf_op jit(solution)/shard_map/ppermute | solution.py:163
  81.0 18.9 %collective-permute-start.4 = (f32[1,11,32,128]{3,2,1,0:T(8,128)S(1)}, f32[1,11,32,128]{3,2,1,0:T(8,128)S(1)}, u32[]{:S(2)}, u32[]{:S(2)}) collective-permute-start(f32[1,11,32,128]{3,2,1,0:T(8,128)S(1)} %get-tuple-element.43), channel_id=1, source_target_pairs={{0,20},{4,24},{8,28},{12,0},{16,4},{20,8},{24,12},{28,16},{1,21},{... | collective-permute-start | bytes 540680 | tf_op jit(solution)/shard_map/ppermute | solution.py:163
  84.5 15.4 %collective-permute-start.5 = (f32[1,11,32,128]{3,2,1,0:T(8,128)S(1)}, f32[1,11,32,128]{3,2,1,0:T(8,128)S(1)}, u32[]{:S(2)}, u32[]{:S(2)}) collective-permute-start(f32[1,11,32,128]{3,2,1,0:T(8,128)S(1)} %get-tuple-element.42), channel_id=1, source_target_pairs={{0,24},{4,28},{8,0},{12,4},{16,8},{20,12},{24,16},{28,20},{1,25},{... | collective-permute-start | bytes 540680 | tf_op jit(solution)/shard_map/ppermute | solution.py:163
  86.4 16.5 %collective-permute-start.6 = (f32[1,11,32,128]{3,2,1,0:T(8,128)S(1)}, f32[1,11,32,128]{3,2,1,0:T(8,128)S(1)}, u32[]{:S(2)}, u32[]{:S(2)}) collective-permute-start(f32[1,11,32,128]{3,2,1,0:T(8,128)S(1)} %get-tuple-element.41), channel_id=1, source_target_pairs={{0,28},{4,0},{8,4},{12,8},{16,12},{20,16},{24,20},{28,24},{1,29},{... | collective-permute-start | bytes 540680 | tf_op jit(solution)/shard_map/ppermute | solution.py:163
  105.5 12.3 %all-to-all-start.1 = ((f32[32,32,128]{2,1,0:T(8,128)}), f32[32,32,128]{2,1,0:T(8,128)S(1)}, u32[]{:S(2)}, u32[]{:S(2)}) async-start(f32[32,32,128]{2,1,0:T(8,128)} %copy.56), calls=%async_computation.1 | async-start | bytes 1048576 | tf_op jit(solution)/shard_map/all_to_all | solution.py:176
  108.9 166.9 %all-reduce.4.cloned.1.call-start = ((), (), s32[]{:S(2)}) async-start(), calls=%async_computation.2 | async-start | bytes 7864320 | tf_op jit(solution)/shard_map/psum | solution.py:211
  125.2 1.4 copy-start.4
  125.9 20.4 %copy-start.14 = (s32[72]{0:T(128)S(1)}, s32[72]{0:T(128)}, u32[]{:S(2)}) copy-start(s32[72]{0:T(128)} %constant.521) | copy-start | bytes 868
  125.9 27.7 %copy-start.13 = (f32[1,128]{1,0:T(1,128)S(1)}, f32[1,128]{1,0:T(1,128)}, u32[]{:S(2)}) copy-start(f32[1,128]{1,0:T(1,128)} %param.20) | copy-start | bytes 1540
  130.3 16.1 %collective-permute-start.10 = (f32[128]{0:T(128)S(1)}, f32[128]{0:T(128)S(1)}, u32[]{:S(2)}, u32[]{:S(2)}) collective-permute-start(f32[128]{0:T(128)S(1)} %get-tuple-element.68), channel_id=1, source_target_pairs={{0,4},{1,5},{2,6},{3,7},{4,8},{5,9},{6,10},{7,11},{8,12},{9,13},{1... | collective-permute-start | bytes 1544 | tf_op jit(solution)/shard_map/ppermute | solution.py:27
  136.1 10.5 %collective-permute-start.11 = (f32[128]{0:T(128)S(1)}, f32[128]{0:T(128)S(1)}, u32[]{:S(2)}, u32[]{:S(2)}) collective-permute-start(f32[128]{0:T(128)S(1)} %get-tuple-element.67), channel_id=1, source_target_pairs={{0,5},{1,6},{2,7},{3,8},{4,9},{5,10},{6,11},{7,12},{8,13},{9,14},{... | collective-permute-start | bytes 1544 | tf_op jit(solution)/shard_map/ppermute | solution.py:27
  136.1 12.0 %collective-permute-start.12 = (f32[128]{0:T(128)S(1)}, f32[128]{0:T(128)S(1)}, u32[]{:S(2)}, u32[]{:S(2)}) collective-permute-start(f32[128]{0:T(128)S(1)} %get-tuple-element.66), channel_id=1, source_target_pairs={{0,6},{1,7},{2,8},{3,9},{4,10},{5,11},{6,12},{7,13},{8,14},{9,15},... | collective-permute-start | bytes 1544 | tf_op jit(solution)/shard_map/ppermute | solution.py:27
  141.3 6.9 %collective-permute-start.13 = (f32[128]{0:T(128)S(1)}, f32[128]{0:T(128)S(1)}, u32[]{:S(2)}, u32[]{:S(2)}) collective-permute-start(f32[128]{0:T(128)S(1)} %get-tuple-element.65), channel_id=1, source_target_pairs={{0,7},{1,8},{2,9},{3,10},{4,11},{5,12},{6,13},{7,14},{8,15},{9,16}... | collective-permute-start | bytes 1544 | tf_op jit(solution)/shard_map/ppermute | solution.py:27
  146.3 6.6 %collective-permute-start.7 = (f32[128]{0:T(128)S(1)}, f32[128]{0:T(128)S(1)}, u32[]{:S(2)}, u32[]{:S(2)}) collective-permute-start(f32[128]{0:T(128)S(1)} %get-tuple-element.64), channel_id=1, source_target_pairs={{0,1},{1,2},{2,3},{3,4},{4,5},{5,6},{6,7},{7,8},{8,9},{9,10},{10,1... | collective-permute-start | bytes 1544 | tf_op jit(solution)/shard_map/ppermute | solution.py:27
  146.4 7.2 %collective-permute-start.8 = (f32[128]{0:T(128)S(1)}, f32[128]{0:T(128)S(1)}, u32[]{:S(2)}, u32[]{:S(2)}) collective-permute-start(f32[128]{0:T(128)S(1)} %get-tuple-element.70), channel_id=1, source_target_pairs={{0,2},{1,3},{2,4},{3,5},{4,6},{5,7},{6,8},{7,9},{8,10},{9,11},{10,... | collective-permute-start | bytes 1544 | tf_op jit(solution)/shard_map/ppermute | solution.py:27
  146.7 6.9 %collective-permute-start.9 = (f32[128]{0:T(128)S(1)}, f32[128]{0:T(128)S(1)}, u32[]{:S(2)}, u32[]{:S(2)}) collective-permute-start(f32[128]{0:T(128)S(1)} %get-tuple-element.69), channel_id=1, source_target_pairs={{0,3},{1,4},{2,5},{3,6},{4,7},{5,8},{6,9},{7,10},{8,11},{9,12},{10... | collective-permute-start | bytes 1544 | tf_op jit(solution)/shard_map/ppermute | solution.py:27
  303.0 16.5 %copy-start.8 = (f32[512,512]{1,0:T(8,128)S(1)}, f32[512,512]{1,0:T(8,128)}, u32[]{:S(2)}) copy-start(f32[512,512]{1,0:T(8,128)} %copy-done.7) | copy-start | bytes 3145732
  389.9 49.4 %copy-start.6 = (f32[512,512]{1,0:T(8,128)}, f32[512,512]{1,0:T(8,128)S(1)}, u32[]{:S(2)}) copy-start(f32[512,512]{1,0:T(8,128)S(1)} %get-tuple-element.139) | copy-start | bytes 3145732
  453.0 7.7 %copy-start.2 = (f32[2304,512]{1,0:T(8,128)S(1)}, f32[2304,512]{1,0:T(8,128)}, u32[]{:S(2)}) copy-start(f32[2304,512]{1,0:T(8,128)} %copy.65) | copy-start | bytes 14155780
  475.8 8.5 %copy-start.1 = (f32[32,128]{1,0:T(8,128)S(1)}, f32[32,128]{1,0:T(8,128)}, u32[]{:S(2)}) copy-start(f32[32,128]{1,0:T(8,128)} %param.21) | copy-start | bytes 49156
  (3 other events, 2.9 us)
Sparse Core Ops, SparseCore 0:
  125.4 150.4 all-reduce.3
